TPU v7x, 128 devices: a whole 4x4x4 slice. The times are simulated.
128 devices in a mesh: beam: 16 (over x_lo, y, core), seg: 8 (over z, x_hi).
Axes of the slice: x: 4 (x_hi: 2, x_lo: 2; x = x_hi * 2 + x_lo), y: 4, z: 4, core: 2. Of those that a mesh axis runs over, the one named last changes fastest.
Arguments:
- voltages: bfloat16 [2, 256, 8, 65536], P(None, 'beam', 'seg'), may hold values from -6 to 6
- surv_taps: bfloat16 [32], replicated, may hold values from -1 to 1
- ref_taps: bfloat16 [32], replicated, may hold values from -1 to 1
- tx_owner: int32 [4], replicated, may hold values from 0 to 255
- delay_start: int32 [4], replicated, may hold values from 0 to 384
- doppler_start: int32 [4], replicated, may hold values from 0 to 128
Outputs:
- maps: float32 [4, 256, 128, 128], P(None, 'beam', 'seg')
All inputs are finite; a program needn't handle non-finite values.
Results may differ from a plain program's by a relative error of at most 0.0027.
Values may be sent and summed in bfloat16 or wider, within the bound.
A program may use at most 128 MiB of HBM per device.

v0:
```python
import jax
import jax.numpy as jnp
from jax import lax
from jax.sharding import PartitionSpec as P

TX = 4
DECIM = 4
TAPS = 32
BLOCK_LEN = 64
BLOCKS = 256
DELAYS = 128
DOPPLER = 128
MAXDELAY = 512


def from_root(value, axis, source):
    kept = jnp.where(lax.axis_index(axis) == source, value, 0).astype(value.dtype)
    return lax.psum(kept, axis)


def band_matrix(taps):
    rows = DECIM * BLOCK_LEN + TAPS - 1
    row_ids = jnp.arange(rows, dtype=jnp.int32)[:, None]
    col_ids = jnp.arange(BLOCK_LEN, dtype=jnp.int32)[None, :]
    offset = DECIM * col_ids + TAPS - 1 - row_ids
    tap_ids = jnp.arange(TAPS, dtype=jnp.int32)
    picked = jnp.where(offset[..., None] == tap_ids, taps.astype(jnp.float32), 0.0)
    return jnp.sum(picked, axis=-1).astype(jnp.bfloat16)


def decimate(raw, taps):
    lead = raw.shape[:-1]
    stride = DECIM * BLOCK_LEN
    count = raw.shape[-1] // stride
    blocks = raw.reshape(lead + (count, stride))
    tail = blocks[..., :-1, stride - (TAPS - 1) :]
    tail = jnp.pad(tail, [(0, 0)] * len(lead) + [(1, 0), (0, 0)])
    extended = jnp.concatenate([tail, blocks], axis=-1)
    filtered = jnp.einsum(
        "...k,km->...m", extended, band_matrix(taps), preferred_element_type=jnp.float32
    )
    return filtered.astype(jnp.bfloat16).reshape(lead + (count * BLOCK_LEN,))


def tables(f_lo):
    ells = jnp.arange(BLOCKS, dtype=jnp.int32)
    freqs = f_lo + jnp.arange(DOPPLER, dtype=jnp.int32) - BLOCKS // 2
    phase = ells[:, None] * freqs[None, :] % BLOCKS
    angle = 2.0 * jnp.pi / BLOCKS * phase.astype(jnp.float32)
    return (jnp.cos(angle).astype(jnp.bfloat16), jnp.sin(angle).astype(jnp.bfloat16))


def partial_einsum(form, left, right):
    return jnp.einsum(form, left, right, preferred_element_type=jnp.float32)


def ambiguity(surv, ref, d_lo, f_lo):
    beams = surv.shape[1]
    segs = surv.shape[2]
    span = BLOCK_LEN + DELAYS - 1
    extra = (DELAYS - 1 + BLOCK_LEN - 1) // BLOCK_LEN
    cos_t, sin_t = tables(f_lo)
    scale = BLOCK_LEN ** (-0.5)

    def one_segment(seg):
        blocks_s = lax.dynamic_index_in_dim(surv, seg, 2, keepdims=False).reshape(
            2, beams, BLOCKS, BLOCK_LEN
        )
        ref_seg = lax.dynamic_index_in_dim(ref, seg, 1, keepdims=False)
        rpad = jnp.pad(ref_seg, ((0, 0), (MAXDELAY, extra * BLOCK_LEN)))
        start = MAXDELAY - (DELAYS - 1) - d_lo
        rwin = lax.dynamic_slice_in_dim(rpad, start, (BLOCKS + extra) * BLOCK_LEN, 1)
        rwin = rwin.reshape(2, BLOCKS + extra, BLOCK_LEN)
        window = jnp.concatenate([rwin[:, e : e + BLOCKS] for e in range(extra + 1)], axis=2)[
            ..., :span
        ]
        tiled = jnp.tile(window, (1, 1, BLOCK_LEN + 1))[..., : BLOCK_LEN * (span + 1)]
        toeplitz = tiled.reshape(2, BLOCKS, BLOCK_LEN, span + 1)[..., :DELAYS]
        s_re, s_im = (blocks_s[0], blocks_s[1])
        u_re, u_im = (toeplitz[0], toeplitz[1])
        c_re = (
            partial_einsum("blm,lmi->bli", s_re, u_re) + partial_einsum("blm,lmi->bli", s_im, u_im)
        ) * scale
        c_im = (
            partial_einsum("blm,lmi->bli", s_im, u_re) - partial_einsum("blm,lmi->bli", s_re, u_im)
        ) * scale
        c_re = c_re[..., ::-1].astype(jnp.bfloat16)
        c_im = c_im[..., ::-1].astype(jnp.bfloat16)
        x_re = partial_einsum("blj,lf->bjf", c_re, cos_t) + partial_einsum(
            "blj,lf->bjf", c_im, sin_t
        )
        x_im = partial_einsum("blj,lf->bjf", c_im, cos_t) - partial_einsum(
            "blj,lf->bjf", c_re, sin_t
        )
        return (x_re * x_re + x_im * x_im) * (1.0 / (4 * BLOCKS))

    powers = lax.map(one_segment, jnp.arange(segs, dtype=jnp.int32))
    return jnp.sum(powers, axis=0)


def shards(voltages, surv_taps, ref_taps, tx_owner, delay_start, doppler_start):
    beams_here = voltages.shape[1]
    surv = decimate(voltages, surv_taps)
    segments_all = lax.axis_size("seg") * voltages.shape[2]
    collected = []
    for trans in range(TX):
        owner = tx_owner[trans]
        root = owner // beams_here
        local_beam = owner % beams_here
        mine = lax.dynamic_index_in_dim(voltages, local_beam, 1, keepdims=False)
        arrived = from_root(mine, "beam", root)
        ref = decimate(arrived, ref_taps)
        power = ambiguity(surv, ref, delay_start[trans], doppler_start[trans])
        summed = lax.psum_scatter(power, "seg", scatter_dimension=1, tiled=True)
        collected.append(summed / segments_all)
    return jnp.stack(collected, axis=0)


def solution(mesh):
    return jax.shard_map(
        shards,
        mesh=mesh,
        in_specs=(P(None, "beam", "seg", None), P(), P(), P(), P(), P()),
        out_specs=P(None, "beam", "seg", None),
        check_vma=False,
    )
```

profile of v0, /device:TPU:0, one launch (start us, length us, event | category | flops | bytes accessed | tf_op | source)
XLA Modules:
  0.0 667.7 jit_solution(16479196598512230570)
XLA Ops:
  18.5 11.2 %fusion.80 = (bf16[2,65536]{1,0:T(2,128)(2,1)S(1)}, bf16[2,65536]{1,0:T(2,128)(2,1)S(1)}, bf16[2,65536]{1,0:T(2,128)(2,1)S(1)}, bf16[2,65536]{1,0:T(2,128)(2,1)S(1)}) fusion(pred[]{:T(512)S(6)} %eq.30, bf16[2,16,1,65536]{3,1,2,0:T(8,128)(2,1)} %param.6, s32[]{:T(128)S(6)} %select_n.176, s32[]{:T(128)S(6)} %select_n.186, pred[]{:T(512)S(6)} %eq.34, ...), kind=kLoop, calls=%fused_computation.98 | loop fusion | flops 524288 | bytes 2097172 | tf_op jit(solution)/shard_map/jit(_where)/select_n | solution.py:17
  39.0 6.3 copy.97
  64.3 91.9 %all-reduce.12.cloned.1.call-done = (bf16[2,1,256,256]{2,3,0,1:T(8,128)(2,1)}, bf16[2,1,256,256]{2,3,0,1:T(8,128)(2,1)}, bf16[2,1,256,256]{2,3,0,1:T(8,128)(2,1)}, bf16[2,1,256,256]{2,3,0,1:T(8,128)(2,1)}) async-done(((bf16[2,1,256,256]{2,3,0,1:T(8,128)(2,1)}, bf16[2,1,256,256]{2,3,0,1:T(8,128)(2,1)}, bf16[2,1,256,256]{2,3,0,1:T(8,128)(2,1)}, bf16[2,1,256,256]{2,3,0,1:T(8,128)(2,1)}), ...) | async-done | bytes 1048592 | tf_op jit(solution)/shard_map/psum | solution.py:18
  162.3 6.2 tile.62
  168.4 14.5 %tile.63 = bf16[2,256,12415]{1,2,0:T(8,128)(2,1)} reshape(bf16[2,256,65,191]{1,3,2,0:T(8,128)(2,1)} %tile.62) | data formatting | bytes 25425920 | tf_op jit(solution)/shard_map/while/body/eval_jaxpr/tile | solution.py:77
  191.3 6.7 %copy.155 = bf16[1,256,64,128]{3,2,1,0:T(8,128)(2,1)} copy(bf16[1,256,64,128]{1,3,2,0:T(8,128)(2,1)} %get-tuple-element.90) | data formatting | bytes 8388608
  205.5 6.2 tile.60
  211.6 14.5 %tile.61 = bf16[2,256,12415]{1,2,0:T(8,128)(2,1)} reshape(bf16[2,256,65,191]{1,3,2,0:T(8,128)(2,1)} %tile.60) | data formatting | bytes 25425920 | tf_op jit(solution)/shard_map/while/body/eval_jaxpr/tile | solution.py:77
  234.5 6.5 copy.153
  249.8 6.2 tile.58
  255.9 14.5 %tile.59 = bf16[2,256,12415]{1,2,0:T(8,128)(2,1)} reshape(bf16[2,256,65,191]{1,3,2,0:T(8,128)(2,1)} %tile.58) | data formatting | bytes 25425920 | tf_op jit(solution)/shard_map/while/body/eval_jaxpr/tile | solution.py:77
  278.8 6.8 %copy.151 = bf16[1,256,64,128]{3,2,1,0:T(8,128)(2,1)} copy(bf16[1,256,64,128]{1,3,2,0:T(8,128)(2,1)} %get-tuple-element.86) | data formatting | bytes 8388608
  294.3 6.6 copy.154
  300.9 5.6 subtract_bitcast_fusion
  332.8 7.0 %copy.152 = bf16[1,256,64,128]{3,2,1,0:T(8,128)(2,1)} copy(bf16[1,256,64,128]{1,3,2,0:T(8,128)(2,1)} %get-tuple-element.87) | data formatting | bytes 8388608
  360.7 6.6 copy.150
  367.3 5.6 subtract_bitcast_fusion.2
  375.6 6.2 tile.56
  381.8 14.5 %tile.57 = bf16[2,256,12415]{1,2,0:T(8,128)(2,1)} reshape(bf16[2,256,65,191]{1,3,2,0:T(8,128)(2,1)} %tile.56) | data formatting | bytes 25425920 | tf_op jit(solution)/shard_map/while/body/eval_jaxpr/tile | solution.py:77
  416.6 6.7 %copy.149 = bf16[1,256,64,128]{3,2,1,0:T(8,128)(2,1)} copy(bf16[1,256,64,128]{1,3,2,0:T(8,128)(2,1)} %get-tuple-element.84) | data formatting | bytes 8388608
  442.2 6.6 copy.148
  489.6 19.4 %reduce-scatter.9.cloned.1.call-done = f32[16,16,128]{2,1,0:T(8,128)} async-done(((f32[16,128,128]{2,1,0:T(8,128)}), f32[16,16,128]{2,1,0:T(8,128)}) %reduce-scatter.9.cloned.1.call-update) | async-done | bytes 131088 | tf_op jit(solution)/shard_map/reduce_scatter | solution.py:114
  510.0 74.1 %reduce-scatter.7.cloned.1.call-done = f32[16,16,128]{2,1,0:T(8,128)} async-done(((f32[16,128,128]{2,1,0:T(8,128)}), f32[16,16,128]{2,1,0:T(8,128)}) %reduce-scatter.7.cloned.1.call-update) | async-done | bytes 131088 | tf_op jit(solution)/shard_map/reduce_scatter | solution.py:114
  585.0 74.2 %reduce-scatter.5.cloned.1.call-done = f32[16,16,128]{2,1,0:T(8,128)} async-done(((f32[16,128,128]{2,1,0:T(8,128)}), f32[16,16,128]{2,1,0:T(8,128)}) %reduce-scatter.5.cloned.1.call-update) | async-done | bytes 131088 | tf_op jit(solution)/shard_map/reduce_scatter | solution.py:114
  (190 shorter events, 214.1 us)
Async XLA Ops:
  6.5 149.7 %all-reduce.12.cloned.1.call-start = ((), (), s32[]{:S(2)}) async-start(), calls=%async_computation.8 | async-start | bytes 2097152 | tf_op jit(solution)/shard_map/psum | solution.py:18
  18.4 15.3 %copy-start.21 = (bf16[32]{0:T(256)(128)(2,1)S(1)}, bf16[32]{0:T(256)(128)(2,1)}, u32[]{:S(2)}) copy-start(bf16[32]{0:T(256)(128)(2,1)} %param.7) | copy-start | bytes 196
  18.5 15.3 %copy-start.22 = (bf16[32]{0:T(256)(128)(2,1)S(1)}, bf16[32]{0:T(256)(128)(2,1)}, u32[]{:S(2)}) copy-start(bf16[32]{0:T(256)(128)(2,1)} %param.8) | copy-start | bytes 196
  33.2 455.5 %reduce-scatter.11.cloned.1.call-start = ((), (), s32[]{:S(2)}) async-start(), calls=%async_computation.7 | async-start | bytes 1179648 | tf_op jit(solution)/shard_map/reduce_scatter | solution.py:114
  52.0 7.5 %copy-start.15 = (s32[4]{0:T(128)S(1)}, s32[4]{0:T(128)}, u32[]{:S(2)}) copy-start(s32[4]{0:T(128)} %param.11) | copy-start | bytes 52
  182.9 4.6 slice-start
  198.0 4.9 copy-start
  226.1 4.6 slice-start.1
  241.0 4.9 copy-start.1
  270.4 4.6 slice-start.2
  285.6 4.9 copy-start.2
  300.9 5.6 copy-start.3
  300.9 5.6 copy-start.11
  332.8 176.3 %reduce-scatter.9.cloned.1.call-start = ((), (), s32[]{:S(2)}) async-start(), calls=%async_computation.6 | async-start | bytes 1179648 | tf_op jit(solution)/shard_map/reduce_scatter | solution.py:114
  339.8 5.5 copy-start.4
  339.8 5.5 copy-start.9
  367.3 5.6 copy-start.5
  367.3 5.6 copy-start.10
  396.3 4.6 slice-start.3
  416.6 6.7 %copy-start.18 = (s32[128]{0:T(128)S(1)}, s32[128]{0:T(128)}, u32[]{:S(2)}) copy-start(s32[128]{0:T(128)} %add_add_fusion.1) | copy-start | bytes 1540
  423.3 4.4 copy-start.6
  435.3 148.8 %reduce-scatter.7.cloned.1.call-start = ((), (), s32[]{:S(2)}) async-start(), calls=%async_computation.5 | async-start | bytes 1179648 | tf_op jit(solution)/shard_map/reduce_scatter | solution.py:114
  469.1 190.1 %reduce-scatter.5.cloned.1.call-start = ((), (), s32[]{:S(2)}) async-start(), calls=%async_computation.4 | async-start | bytes 1179648 | tf_op jit(solution)/shard_map/reduce_scatter | solution.py:114
  477.3 6.7 %copy-start.16 = (s32[128]{0:T(128)S(1)}, s32[128]{0:T(128)}, u32[]{:S(2)}) copy-start(s32[128]{0:T(128)} %add_add_fusion.3) | copy-start | bytes 1540
  (8 other events, 26.5 us)
Sparse Core Ops, SparseCore 0:
  33.3 122.8 all-reduce.11
  332.9 73.6 reduce-scatter.10
  435.4 73.5 reduce-scatter.8
  512.5 71.5 reduce-scatter.6
  587.5 71.5 reduce-scatter.4
where the time goes:
time: 678 us; the launch traced here: 668 us
  waiting for transfers between devices  260 us (38%)
  local copies, waits for them, and re-layouts  242 us (36%)
  matrix products  96.6 us (14%)
  other arithmetic  39.1 us (6%)
  between operations  29.2 us (4%)
    reduce_scatter x4, waiting for transfers between devices, shards(): summed = lax.psum_scatter(power, 'seg', scatter_dimension=1, tiled=True)  168 us
    psum x1, waiting for transfers between devices, from_root(): return lax.psum(kept, axis)  91.9 us
    dot_general x32, matrix products, partial_einsum(): return jnp.einsum(form, left, right, preferred_element_type=jnp.float32)  89.7 us
    another operation x8, local copies, waits for them, and re-layouts, one_segment(): jnp.tile(window, (1, 1, BLOCK_LEN + 1))[..., :BLOCK_LEN * (span + 1)]  82.7 us
    unnamed x59, local copies, waits for them, and re-layouts  58.7 us
    another operation x8, local copies, waits for them, and re-layouts  33.2 us
    slice x8, local copies, waits for them, and re-layouts, one_segment(): jnp.tile(window, (1, 1, BLOCK_LEN + 1))[..., :BLOCK_LEN * (span + 1)]  18.3 us
    slice x4, local copies, waits for them, and re-layouts, one_segment(): u_re, u_im = (toeplitz[0], toeplitz[1])  15.1 us
  transfers between devices with their start and end apart: 5, of which 4 were waited for; matrix products, arithmetic and copies ran while one was open for 27% of the time, Pallas kernels for 0%

commit v1 on v0

--- a/solution.py
+++ b/solution.py
@@ -15,7 +15,13 @@
 
 def from_root(value, axis, source):
     kept = jnp.where(lax.axis_index(axis) == source, value, 0).astype(value.dtype)
-    return lax.psum(kept, axis)
+
+    def make_the_bars(s0, chip_axis):
+        x_now = lax.all_gather(s0, chip_axis)
+        front = jnp.sum(x_now, axis=0)
+        return front
+
+    return make_the_bars(kept, axis)
 
 
 def band_matrix(taps):

time: 678 us -> 776 us (1.14)
  other arithmetic: 39.1 us -> 162 us
  waiting for transfers between devices: 260 us -> 222 us
  local copies, waits for them, and re-layouts: 242 us -> 264 us
    all_gather x0 -> x4, other arithmetic: none -> 103 us  [make_the_bars(): x_now = lax.all_gather(s0, chip_axis)]
    psum x1 -> x0, waiting for transfers between devices: 91.9 us -> none  [from_root(): return lax.psum(kept, axis)]
    all_gather x0 -> x4, waiting for transfers between devices: none -> 52.4 us  [make_the_bars(): x_now = lax.all_gather(s0, chip_axis)]
    all_gather x0 -> x4, local copies, waits for them, and re-layouts: none -> 25.1 us  [make_the_bars(): x_now = lax.all_gather(s0, chip_axis)]
    reduce_sum x0 -> x4, other arithmetic: none -> 24.1 us  [make_the_bars(): front = jnp.sum(x_now, axis=0)]
    unnamed x59 -> x55, local copies, waits for them, and re-layouts: 58.7 us -> 58.9 us
  transfers between devices with their start and end apart: 5 -> 8, of which waited for: 4 -> 6; matrix products, arithmetic and copies ran while one was open for 27% -> 53% of each run, Pallas kernels for 0% -> 0%
where the time goes in v1:
time: 776 us; the launch traced here: 769 us
  local copies, waits for them, and re-layouts  264 us (34%)
  waiting for transfers between devices  222 us (29%)
  other arithmetic  162 us (21%)
  matrix products  90 us (12%)
  between operations  29.8 us (4%)
    reduce_scatter x4, waiting for transfers between devices, shards(): summed = lax.psum_scatter(power, 'seg', scatter_dimension=1, tiled=True)  168 us
    all_gather x4, other arithmetic, make_the_bars(): x_now = lax.all_gather(s0, chip_axis)  103 us
    dot_general x32, matrix products, partial_einsum(): return jnp.einsum(form, left, right, preferred_element_type=jnp.float32)  85 us
    another operation x8, local copies, waits for them, and re-layouts, one_segment(): jnp.tile(window, (1, 1, BLOCK_LEN + 1))[..., :BLOCK_LEN * (span + 1)]  82.9 us
    unnamed x55, local copies, waits for them, and re-layouts  58.9 us
    all_gather x4, waiting for transfers between devices, make_the_bars(): x_now = lax.all_gather(s0, chip_axis)  52.4 us
    another operation x8, local copies, waits for them, and re-layouts  33.3 us
    all_gather x4, local copies, waits for them, and re-layouts, make_the_bars(): x_now = lax.all_gather(s0, chip_axis)  25.1 us
  transfers between devices with their start and end apart: 8, of which 6 were waited for; matrix products, arithmetic and copies ran while one was open for 53% of the time, Pallas kernels for 0%

profile of v1, /device:TPU:0, one launch (start us, length us, event | category | flops | bytes accessed | tf_op | source)
XLA Modules:
  0.0 769.1 jit_solution(13433049149719868239)
XLA Ops:
  18.5 7.4 broadcast_select_fusion.3
  59.1 21.4 %all-gather.11.cloned.1.call-done = bf16[32,1,1,65536]{3,2,1,0:T(2,128)(2,1)} async-done(((bf16[2,1,1,65536]{3,2,1,0:T(2,128)(2,1)}), bf16[32,1,1,65536]{3,2,1,0:T(2,128)(2,1)}) %all-gather.11.cloned.1.call-update) | async-done | bytes 4194320 | tf_op jit(solution)/shard_map/all_gather | solution.py:20
  80.6 25.9 %reduce.13 = bf16[32,65536]{1,0:T(8,128)(2,1)} reduce(bf16[32,1,1,65536]{3,2,1,0:T(2,128)(2,1)} %all-gather.11.cloned.1.call-done, bf16[]{:T(256)} %constant.253), dimensions={1,2}, to_apply=%all-gather.1.reduce_sub_computation | reduce | bytes 8388610 | tf_op jit(solution)/shard_map/all_gather | solution.py:20
  118.9 16.4 %all-gather.15.cloned.1.call-done = bf16[32,1,1,65536]{3,2,1,0:T(2,128)(2,1)} async-done(((bf16[2,1,1,65536]{3,2,1,0:T(2,128)(2,1)}), bf16[32,1,1,65536]{3,2,1,0:T(2,128)(2,1)}) %all-gather.15.cloned.1.call-update) | async-done | bytes 4194320 | tf_op jit(solution)/shard_map/all_gather | solution.py:20
  135.3 25.8 %reduce.15 = bf16[32,65536]{1,0:T(8,128)(2,1)} reduce(bf16[32,1,1,65536]{3,2,1,0:T(2,128)(2,1)} %all-gather.15.cloned.1.call-done, bf16[]{:T(256)} %constant.253), dimensions={1,2}, to_apply=%all-gather.3.reduce_sub_computation | reduce | bytes 8388610 | tf_op jit(solution)/shard_map/all_gather | solution.py:20
  161.0 6.7 reshape.283
  175.4 14.6 %all-gather.13.cloned.1.call-done = bf16[32,1,1,65536]{3,2,1,0:T(2,128)(2,1)} async-done(((bf16[2,1,1,65536]{3,2,1,0:T(2,128)(2,1)}), bf16[32,1,1,65536]{3,2,1,0:T(2,128)(2,1)}) %all-gather.13.cloned.1.call-update) | async-done | bytes 4194320 | tf_op jit(solution)/shard_map/all_gather | solution.py:20
  190.0 25.8 %reduce.14 = bf16[32,65536]{1,0:T(8,128)(2,1)} reduce(bf16[32,1,1,65536]{3,2,1,0:T(2,128)(2,1)} %all-gather.13.cloned.1.call-done, bf16[]{:T(256)} %constant.253), dimensions={1,2}, to_apply=%all-gather.2.reduce_sub_computation | reduce | bytes 8388610 | tf_op jit(solution)/shard_map/all_gather | solution.py:20
  236.8 14.6 %tile.63 = bf16[2,256,12415]{1,2,0:T(8,128)(2,1)} reshape(bf16[2,256,65,191]{1,3,2,0:T(8,128)(2,1)} %tile.62) | data formatting | bytes 25425920 | tf_op jit(solution)/shard_map/while/body/eval_jaxpr/tile | solution.py:83
  259.7 6.5 copy.237
  272.4 14.7 %tile.59 = bf16[2,256,12415]{1,2,0:T(8,128)(2,1)} reshape(bf16[2,256,65,191]{1,3,2,0:T(8,128)(2,1)} %tile.58) | data formatting | bytes 25425920 | tf_op jit(solution)/shard_map/while/body/eval_jaxpr/tile | solution.py:83
  295.4 6.6 copy.231
  308.1 14.5 %tile.61 = bf16[2,256,12415]{1,2,0:T(8,128)(2,1)} reshape(bf16[2,256,65,191]{1,3,2,0:T(8,128)(2,1)} %tile.60) | data formatting | bytes 25425920 | tf_op jit(solution)/shard_map/while/body/eval_jaxpr/tile | solution.py:83
  330.9 6.9 copy.234
  355.6 25.8 %reduce.12 = bf16[32,65536]{1,0:T(8,128)(2,1)} reduce(bf16[32,1,1,65536]{3,2,1,0:T(2,128)(2,1)} %all-gather.9.cloned.1.call-done, bf16[]{:T(256)} %constant.253), dimensions={1,2}, to_apply=%all-gather.reduce_sub_computation | reduce | bytes 8388610 | tf_op jit(solution)/shard_map/all_gather | solution.py:20
  394.9 6.6 copy.236
  433.7 6.8 copy.230
  461.4 6.6 copy.233
  482.4 14.5 %tile.57 = bf16[2,256,12415]{1,2,0:T(8,128)(2,1)} reshape(bf16[2,256,65,191]{1,3,2,0:T(8,128)(2,1)} %tile.56) | data formatting | bytes 25425920 | tf_op jit(solution)/shard_map/while/body/eval_jaxpr/tile | solution.py:83
  517.2 6.9 copy.228
  543.1 6.5 copy.227
  590.5 19.4 %reduce-scatter.7.cloned.1.call-done = f32[16,16,128]{2,1,0:T(8,128)} async-done(((f32[16,128,128]{2,1,0:T(8,128)}), f32[16,16,128]{2,1,0:T(8,128)}) %reduce-scatter.7.cloned.1.call-update) | async-done | bytes 131088 | tf_op jit(solution)/shard_map/reduce_scatter | solution.py:120
  610.8 74.3 %reduce-scatter.9.cloned.1.call-done = f32[16,16,128]{2,1,0:T(8,128)} async-done(((f32[16,128,128]{2,1,0:T(8,128)}), f32[16,16,128]{2,1,0:T(8,128)}) %reduce-scatter.9.cloned.1.call-update) | async-done | bytes 131088 | tf_op jit(solution)/shard_map/reduce_scatter | solution.py:120
  686.0 74.3 %reduce-scatter.5.cloned.1.call-done = f32[16,16,128]{2,1,0:T(8,128)} async-done(((f32[16,128,128]{2,1,0:T(8,128)}), f32[16,16,128]{2,1,0:T(8,128)}) %reduce-scatter.5.cloned.1.call-update) | async-done | bytes 131088 | tf_op jit(solution)/shard_map/reduce_scatter | solution.py:120
  (207 shorter events, 289.9 us)
Async XLA Ops:
  6.5 21.8 %copy-start.14 = (s32[4]{0:T(128)S(1)}, s32[4]{0:T(128)}, u32[]{:S(2)}) copy-start(s32[4]{0:T(128)} %param.10) | copy-start | bytes 52
  6.5 27.3 %copy-start.19 = (bf16[32]{0:T(256)(128)(2,1)S(1)}, bf16[32]{0:T(256)(128)(2,1)}, u32[]{:S(2)}) copy-start(bf16[32]{0:T(256)(128)(2,1)} %param.7) | copy-start | bytes 196
  6.5 27.3 %copy-start.20 = (bf16[32]{0:T(256)(128)(2,1)S(1)}, bf16[32]{0:T(256)(128)(2,1)}, u32[]{:S(2)}) copy-start(bf16[32]{0:T(256)(128)(2,1)} %param.8) | copy-start | bytes 196
  6.5 27.4 %copy-start.15 = (s32[4]{0:T(128)S(1)}, s32[4]{0:T(128)}, u32[]{:S(2)}) copy-start(s32[4]{0:T(128)} %param.11) | copy-start | bytes 52
  6.5 74.0 %all-gather.11.cloned.1.call-start = ((), (), s32[]{:S(2)}) async-start(), calls=%async_computation.9 | async-start | bytes 8912896 | tf_op jit(solution)/shard_map/all_gather | solution.py:20
  25.9 109.4 %all-gather.15.cloned.1.call-start = ((), (), s32[]{:S(2)}) async-start(), calls=%async_computation.11 | async-start | bytes 8912896 | tf_op jit(solution)/shard_map/all_gather | solution.py:20
  26.6 163.4 %all-gather.13.cloned.1.call-start = ((), (), s32[]{:S(2)}) async-start(), calls=%async_computation.10 | async-start | bytes 8912896 | tf_op jit(solution)/shard_map/all_gather | solution.py:20
  27.4 328.2 %all-gather.9.cloned.1.call-start = ((), (), s32[]{:S(2)}) async-start(), calls=%async_computation.8 | async-start | bytes 8912896 | tf_op jit(solution)/shard_map/all_gather | solution.py:20
  27.9 561.6 %reduce-scatter.11.cloned.1.call-start = ((), (), s32[]{:S(2)}) async-start(), calls=%async_computation.7 | async-start | bytes 1179648 | tf_op jit(solution)/shard_map/reduce_scatter | solution.py:120
  251.4 4.6 slice-start
  287.1 4.6 slice-start.1
  337.9 4.9 copy-start
  401.5 5.6 copy-start.3
  401.5 5.6 copy-start.11
  433.7 176.2 %reduce-scatter.7.cloned.1.call-start = ((), (), s32[]{:S(2)}) async-start(), calls=%async_computation.5 | async-start | bytes 1179648 | tf_op jit(solution)/shard_map/reduce_scatter | solution.py:120
  440.5 5.6 copy-start.4
  440.5 5.6 copy-start.10
  467.9 5.6 copy-start.5
  467.9 5.6 copy-start.9
  496.9 4.6 slice-start.3
  517.2 7.0 copy-start.18
  536.2 148.9 %reduce-scatter.9.cloned.1.call-start = ((), (), s32[]{:S(2)}) async-start(), calls=%async_computation.6 | async-start | bytes 1179648 | tf_op jit(solution)/shard_map/reduce_scatter | solution.py:120
  570.0 190.3 %reduce-scatter.5.cloned.1.call-start = ((), (), s32[]{:S(2)}) async-start(), calls=%async_computation.4 | async-start | bytes 1179648 | tf_op jit(solution)/shard_map/reduce_scatter | solution.py:120
  578.2 6.7 copy-start.16
  (9 other events, 31.6 us)
Sparse Core Ops, SparseCore 0:
  26.0 54.5 all-gather.10
  82.3 52.9 all-gather.14
  137.0 52.9 all-gather.12
  191.6 52.9 all-gather.8
  433.8 73.5 reduce-scatter.10
  536.4 73.4 reduce-scatter.6
  613.5 71.5 reduce-scatter.8
  688.7 71.5 reduce-scatter.4
